TPU v7x, 32 devices: a whole 2x2x4 slice. The times are simulated.
32 devices in a mesh: gx: 8 (over y, x, core), gy: 4 (over z).
Axes of the slice: x: 2, y: 2, z: 4, core: 2. Of those that a mesh axis runs over, the one named last changes fastest.
Arguments:
- phase_pops: float32 [15, 16, 16, 512], P(None, 'gx', None, 'gy'), may hold values from 0 to 0.1
- flow_pops: float32 [19, 16, 16, 512], P(None, 'gx', None, 'gy'), may hold values from 0 to 0.1
- solid_flags: int32 [16, 16, 512], P('gx', None, 'gy'), may hold values 0 or 1
Outputs:
- phase_out: float32 [15, 16, 16, 512], P(None, 'gx', None, 'gy')
- flow_out: float32 [19, 16, 16, 512], P(None, 'gx', None, 'gy')
All inputs are finite; a program needn't handle non-finite values. No bound on the sum of `solid_flags` on one device may be relied on, other than what follows from the above.
Results may differ from a plain program's by a relative error of at most 0.0001.
Values sent between devices are 32-bit elements; how exact they have to be, the bound alone decides.
A program may use at most 64 MiB of HBM per device.

v0:
```python
import jax
import jax.numpy as jnp
from jax import lax
from jax.sharding import PartitionSpec as P

STEPS = 2


PHASE_VELOCITIES = [
    (0, 0, 0),
    (1, 0, 0),
    (-1, 0, 0),
    (0, 1, 0),
    (0, -1, 0),
    (0, 0, 1),
    (0, 0, -1),
    (1, 1, 1),
    (1, 1, -1),
    (1, -1, 1),
    (1, -1, -1),
    (-1, 1, 1),
    (-1, 1, -1),
    (-1, -1, 1),
    (-1, -1, -1),
]
PHASE_WEIGHTS = [2.0 / 9.0] + [1.0 / 9.0] * 6 + [1.0 / 72.0] * 8
FLOW_VELOCITIES = [
    (0, 0, 0),
    (1, 0, 0),
    (-1, 0, 0),
    (0, 1, 0),
    (0, -1, 0),
    (0, 0, 1),
    (0, 0, -1),
    (1, 1, 0),
    (1, -1, 0),
    (-1, 1, 0),
    (-1, -1, 0),
    (1, 0, 1),
    (1, 0, -1),
    (-1, 0, 1),
    (-1, 0, -1),
    (0, 1, 1),
    (0, 1, -1),
    (0, -1, 1),
    (0, -1, -1),
]
FLOW_WEIGHTS = [1.0 / 3.0] + [1.0 / 18.0] * 6 + [1.0 / 36.0] * 12
SURFACE_TENSION = 0.05
INTERFACE_WIDTH = 4.0
GRADIENT_FLOOR = 0.1
PHASE_LAMBDA = 0.3
PHASE_RELAX = 0.8
PHASE_FORWARD = [number for number in range(15) if PHASE_VELOCITIES[number][0] == 1]
PHASE_BACKWARD = [number for number in range(15) if PHASE_VELOCITIES[number][0] == -1]
PHASE_UPWARD = [number for number in range(15) if PHASE_VELOCITIES[number][1] == 1]
PHASE_DOWNWARD = [number for number in range(15) if PHASE_VELOCITIES[number][1] == -1]
PACKED_FORWARD = [0] + [number + 1 for number in range(19) if FLOW_VELOCITIES[number][0] == 1]
PACKED_BACKWARD = [0] + [number + 1 for number in range(19) if FLOW_VELOCITIES[number][0] == -1]
PACKED_UPWARD = [0] + [number + 1 for number in range(19) if FLOW_VELOCITIES[number][1] == 1]
PACKED_DOWNWARD = [0] + [number + 1 for number in range(19) if FLOW_VELOCITIES[number][1] == -1]


def shifted(block, axis, distance):
    devices = range(lax.axis_size(axis))
    route = [((i - distance) % len(devices), i) for i in devices]
    return lax.ppermute(block, axis, route)


def reverse_of(velocities):
    return [velocities.index((-vector[0], -vector[1], -vector[2])) for vector in velocities]


def relax(phase_read, flow_read, phase_field, neighbours, solid_cells):
    gradient = []
    for coordinate in range(3):
        total = jnp.zeros_like(phase_field)
        for number in range(19):
            if FLOW_VELOCITIES[number][coordinate] != 0:
                total = (
                    total
                    + FLOW_WEIGHTS[number]
                    * FLOW_VELOCITIES[number][coordinate]
                    * neighbours[number]
                )
        gradient.append(3.0 * total)
    laplacian = jnp.zeros_like(phase_field)
    for number in range(1, 19):
        laplacian = laplacian + FLOW_WEIGHTS[number] * (neighbours[number] - phase_field)
    laplacian = 6.0 * laplacian
    magnitude = jnp.sqrt(gradient[0] ** 2 + gradient[1] ** 2 + gradient[2] ** 2)
    scaling = 1.0 / jnp.maximum(magnitude, GRADIENT_FLOOR)
    normal = [component * scaling for component in gradient]
    clipped = jnp.clip(phase_field, 0.0, 1.0)
    density = 1.0 + 2.0 * clipped
    relax_time = 0.6 + 0.4 * clipped
    beta_value = 12.0 * SURFACE_TENSION / INTERFACE_WIDTH
    kappa_value = 1.5 * SURFACE_TENSION * INTERFACE_WIDTH
    potential = (
        4.0 * beta_value * phase_field * (phase_field - 1.0) * (phase_field - 0.5)
        - kappa_value * laplacian
    )
    force_terms = [potential * component for component in gradient]
    pressure = jnp.sum(flow_read, axis=0)
    velocity = []
    for coordinate in range(3):
        moment = 0.5 * force_terms[coordinate]
        for number in range(19):
            if FLOW_VELOCITIES[number][coordinate] != 0:
                moment = moment + FLOW_VELOCITIES[number][coordinate] * flow_read[number]
        velocity.append(moment / density)
    speed_sq = velocity[0] ** 2 + velocity[1] ** 2 + velocity[2] ** 2
    force_factor = 3.0 * (1.0 - 0.5 / relax_time) / density
    flow_reverse = reverse_of(FLOW_VELOCITIES)
    flow_post = []
    for number in range(19):
        vector = FLOW_VELOCITIES[number]
        weight = FLOW_WEIGHTS[number]
        along = vector[0] * velocity[0] + vector[1] * velocity[1] + vector[2] * velocity[2]
        along_force = (
            vector[0] * force_terms[0] + vector[1] * force_terms[1] + vector[2] * force_terms[2]
        )
        equilibrium = weight * (pressure + 3.0 * along + 4.5 * along * along - 1.5 * speed_sq)
        current = flow_read[number]
        post_value = (
            current - (current - equilibrium) / relax_time + weight * force_factor * along_force
        )
        flow_post.append(jnp.where(solid_cells, flow_read[flow_reverse[number]], post_value))
    phase_reverse = reverse_of(PHASE_VELOCITIES)
    interface = PHASE_LAMBDA * phase_field * (1.0 - phase_field)
    phase_post = []
    for number in range(15):
        vector = PHASE_VELOCITIES[number]
        weight = PHASE_WEIGHTS[number]
        along = vector[0] * velocity[0] + vector[1] * velocity[1] + vector[2] * velocity[2]
        along_normal = vector[0] * normal[0] + vector[1] * normal[1] + vector[2] * normal[2]
        equilibrium = weight * (phase_field * (1.0 + 3.0 * along) + interface * along_normal)
        current = phase_read[number]
        post_value = current - (current - equilibrium) / PHASE_RELAX
        phase_post.append(jnp.where(solid_cells, phase_read[phase_reverse[number]], post_value))
    return (jnp.stack(phase_post), jnp.stack(flow_post))


def place_layers(lateral, forward_rows, backward_rows, ahead_rows, behind):
    empty_layer = jnp.zeros_like(lateral[:, :1])
    left_layer = empty_layer.at[jnp.array(forward_rows)].set(ahead_rows)
    right_layer = empty_layer.at[jnp.array(backward_rows)].set(behind)
    return jnp.concatenate([left_layer, lateral, right_layer], axis=1)


def with_rims(stacked, forward_rows, backward_rows, upward_rows, downward_rows):
    upper = shifted(stacked[jnp.array(upward_rows), :, :, -1:], "gy", 1)
    lower = shifted(stacked[jnp.array(downward_rows), :, :, :1], "gy", -1)
    empty_column = jnp.zeros_like(stacked[:, :, :, :1])
    left_column = empty_column.at[jnp.array(upward_rows)].set(upper)
    right_column = empty_column.at[jnp.array(downward_rows)].set(lower)
    lateral = jnp.concatenate([left_column, stacked, right_column], axis=3)
    ahead_rows = shifted(lateral[jnp.array(forward_rows), -1:], "gx", 1)
    behind = shifted(lateral[jnp.array(backward_rows), :1], "gx", -1)
    return place_layers(lateral, forward_rows, backward_rows, ahead_rows, behind)


def pull_plane(component, vector, width_x, width_y):
    window = component[
        1 - vector[0] : 1 - vector[0] + width_x, :, 1 - vector[1] : 1 - vector[1] + width_y
    ]
    return jnp.roll(window, vector[2], axis=1)


def shards(phase_pops, flow_pops, solid_flags):
    solid_cells = solid_flags > 0
    width_x = phase_pops.shape[1]
    width_y = phase_pops.shape[3]
    for step in range(STEPS):
        padded = with_rims(phase_pops, PHASE_FORWARD, PHASE_BACKWARD, PHASE_UPWARD, PHASE_DOWNWARD)
        phase_read = jnp.stack(
            [
                pull_plane(padded[number], PHASE_VELOCITIES[number], width_x, width_y)
                for number in range(15)
            ]
        )
        phase_field = jnp.sum(phase_read, axis=0)
        packed = with_rims(
            jnp.concatenate([phase_field[None], flow_pops], axis=0),
            PACKED_FORWARD,
            PACKED_BACKWARD,
            PACKED_UPWARD,
            PACKED_DOWNWARD,
        )
        flow_read = jnp.stack(
            [
                pull_plane(packed[number + 1], FLOW_VELOCITIES[number], width_x, width_y)
                for number in range(19)
            ]
        )
        neighbours = [
            pull_plane(packed[0], (-vector[0], -vector[1], -vector[2]), width_x, width_y)
            for vector in FLOW_VELOCITIES
        ]
        phase_pops, flow_pops = relax(phase_read, flow_read, phase_field, neighbours, solid_cells)
    return (phase_pops, flow_pops)


def solution(mesh):
    placed = (P(None, "gx", None, "gy"), P(None, "gx", None, "gy"), P("gx", None, "gy"))
    return jax.shard_map(
        shards,
        mesh=mesh,
        in_specs=placed,
        out_specs=(P(None, "gx", None, "gy"), P(None, "gx", None, "gy")),
        check_vma=False,
    )
```

profile of v0, /device:TPU:0, one launch (start us, length us, event | category | flops | bytes accessed | tf_op | source)
XLA Modules:
  0.0 87.6 jit_solution(8480701495218105742)
XLA Ops:
  0.7 2.5 %copy.141 = f32[15,2,16,128]{2,1,3,0:T(2,128)S(1)} copy(f32[15,2,16,128]{3,2,1,0:T(8,128)} %param.35) | data formatting | bytes 491520 | tf_op args[0]
  3.8 3.1 %collective-permute-start = (f32[5,2,16,1]{2,1,0,3:T(2,128)S(1)}, f32[5,2,16,1]{2,1,0,3:T(2,128)S(1)}, u32[]{:S(2)}, u32[]{:S(2)}) collective-permute-start(f32[5,2,16,1]{2,1,0,3:T(2,128)S(1)} %bitcast.381), channel_id=1, source_target_pairs={{3,0},{0,1},{1,2},{2,3},{7,4},{4,5},{5,6},{6,7},{11,8},{8,9},{9,10... | collective-permute-start | bytes 1928 | tf_op jit(solution)/shard_map/ppermute | solution.py:67
  7.5 2.1 %collective-permute-start.1 = (f32[5,2,16,1]{2,1,0,3:T(2,128)S(1)}, f32[5,2,16,1]{2,1,0,3:T(2,128)S(1)}, u32[]{:S(2)}, u32[]{:S(2)}) collective-permute-start(f32[5,2,16,1]{2,1,0,3:T(2,128)S(1)} %bitcast.379), channel_id=1, source_target_pairs={{1,0},{2,1},{3,2},{0,3},{5,4},{6,5},{7,6},{4,7},{9,8},{10,9},{11,1... | collective-permute-start | bytes 1928 | tf_op jit(solution)/shard_map/ppermute | solution.py:67
  9.6 0.9 %collective-permute-done = f32[5,2,16,1]{2,1,0,3:T(2,128)S(1)} collective-permute-done((f32[5,2,16,1]{2,1,0,3:T(2,128)S(1)}, f32[5,2,16,1]{2,1,0,3:T(2,128)S(1)}, u32[]{:S(2)}, u32[]{:S(2)}) %collective-permute-start) | collective-permute-done | bytes 672 | tf_op jit(solution)/shard_map/ppermute | solution.py:67
  13.3 1.1 %collective-permute-start.3 = (f32[5,1,16,130]{3,2,0,1:T(8,128)S(1)}, f32[5,1,16,130]{3,2,0,1:T(8,128)S(1)}, u32[]{:S(2)}, u32[]{:S(2)}) collective-permute-start(f32[5,1,16,130]{3,2,0,1:T(8,128)S(1)} %bitcast.365), channel_id=1, source_target_pairs={{4,0},{8,4},{12,8},{16,12},{20,16},{24,20},{28,24},{0,28},{5,1},{9... | collective-permute-start | bytes 124808 | tf_op jit(solution)/shard_map/ppermute | solution.py:67
  15.0 1.4 %collective-permute-done.3 = f32[5,1,16,130]{3,2,0,1:T(8,128)S(1)} collective-permute-done((f32[5,1,16,130]{3,2,0,1:T(8,128)S(1)}, f32[5,1,16,130]{3,2,0,1:T(8,128)S(1)}, u32[]{:S(2)}, u32[]{:S(2)}) %collective-permute-start.3) | collective-permute-done | bytes 41632 | tf_op jit(solution)/shard_map/ppermute | solution.py:67
  17.2 2.6 %collective-permute-done.2 = f32[5,1,16,130]{3,2,0,1:T(8,128)S(1)} collective-permute-done((f32[5,1,16,130]{3,2,0,1:T(8,128)S(1)}, f32[5,1,16,130]{3,2,0,1:T(8,128)S(1)}, u32[]{:S(2)}, u32[]{:S(2)}) %collective-permute-start.2) | collective-permute-done | bytes 41632 | tf_op jit(solution)/shard_map/ppermute | solution.py:67
  22.6 1.3 %copy.146 = f32[20,2,16,128]{2,1,3,0:T(2,128)S(1)} copy(f32[20,2,16,128]{3,2,1,0:T(8,128)S(1)} %pad_maximum_fusion.8) | data formatting | bytes 655360 | tf_op jit(solution)/shard_map/concatenate | solution.py:184
  25.9 3.2 %collective-permute-start.5 = (f32[6,2,16,1]{2,1,0,3:T(2,128)S(1)}, f32[6,2,16,1]{2,1,0,3:T(2,128)S(1)}, u32[]{:S(2)}, u32[]{:S(2)}) collective-permute-start(f32[6,2,16,1]{2,1,0,3:T(2,128)S(1)} %bitcast.373), channel_id=1, source_target_pairs={{1,0},{2,1},{3,2},{0,3},{5,4},{6,5},{7,6},{4,7},{9,8},{10,9},{11,1... | collective-permute-start | bytes 2312 | tf_op jit(solution)/shard_map/ppermute | solution.py:67
  29.1 0.9 %collective-permute-done.4 = f32[6,2,16,1]{2,1,0,3:T(2,128)S(1)} collective-permute-done((f32[6,2,16,1]{2,1,0,3:T(2,128)S(1)}, f32[6,2,16,1]{2,1,0,3:T(2,128)S(1)}, u32[]{:S(2)}, u32[]{:S(2)}) %collective-permute-start.4) | collective-permute-done | bytes 800 | tf_op jit(solution)/shard_map/ppermute | solution.py:67
  34.4 1.6 %collective-permute-done.7 = f32[6,1,16,130]{3,2,0,1:T(8,128)S(1)} collective-permute-done((f32[6,1,16,130]{3,2,0,1:T(8,128)S(1)}, f32[6,1,16,130]{3,2,0,1:T(8,128)S(1)}, u32[]{:S(2)}, u32[]{:S(2)}) %collective-permute-start.7) | collective-permute-done | bytes 49952 | tf_op jit(solution)/shard_map/ppermute | solution.py:67
  36.7 2.1 %collective-permute-done.6 = f32[6,1,16,130]{3,2,0,1:T(8,128)S(1)} collective-permute-done((f32[6,1,16,130]{3,2,0,1:T(8,128)S(1)}, f32[6,1,16,130]{3,2,0,1:T(8,128)S(1)}, u32[]{:S(2)}, u32[]{:S(2)}) %collective-permute-start.6) | collective-permute-done | bytes 49952 | tf_op jit(solution)/shard_map/ppermute | solution.py:67
  42.2 1.0 %constant_dynamic-update-slice_fusion.14 = (f32[15,2,16,128]{3,2,1,0:T(8,128)S(1)}, f32[2,16,128]{2,1,0:T(8,128)S(1)}, f32[2,16,128]{2,1,0:T(8,128)S(1)}, f32[2,...) fusion(f32[2,16,128]{2,1,0:T(8,128)S(1)} %add_add_fusion.3, ...), kind=kLoop, calls=%fused_computation.55 | loop fusion | flops 888831 | bytes 823296
  44.1 1.0 %copy.152 = f32[15,2,16,128]{2,1,3,0:T(2,128)S(1)} copy(f32[15,2,16,128]{3,2,1,0:T(8,128)S(1)} %constant_dynamic-update-slice_fusion) | data formatting | bytes 491520 | tf_op jit(solution)/shard_map/stack | solution.py:141
  46.4 3.9 %collective-permute-start.9 = (f32[5,2,16,1]{2,1,0,3:T(2,128)S(1)}, f32[5,2,16,1]{2,1,0,3:T(2,128)S(1)}, u32[]{:S(2)}, u32[]{:S(2)}) collective-permute-start(f32[5,2,16,1]{2,1,0,3:T(2,128)S(1)} %bitcast.378), channel_id=1, source_target_pairs={{1,0},{2,1},{3,2},{0,3},{5,4},{6,5},{7,6},{4,7},{9,8},{10,9},{11,1... | collective-permute-start | bytes 1928 | tf_op jit(solution)/shard_map/ppermute | solution.py:67
  50.2 0.9 %collective-permute-done.8 = f32[5,2,16,1]{2,1,0,3:T(2,128)S(1)} collective-permute-done((f32[5,2,16,1]{2,1,0,3:T(2,128)S(1)}, f32[5,2,16,1]{2,1,0,3:T(2,128)S(1)}, u32[]{:S(2)}, u32[]{:S(2)}) %collective-permute-start.8) | collective-permute-done | bytes 672 | tf_op jit(solution)/shard_map/ppermute | solution.py:67
  54.6 2.7 %collective-permute-start.11 = (f32[5,1,16,130]{3,2,0,1:T(8,128)S(1)}, f32[5,1,16,130]{3,2,0,1:T(8,128)S(1)}, u32[]{:S(2)}, u32[]{:S(2)}) collective-permute-start(f32[5,1,16,130]{3,2,0,1:T(8,128)S(1)} %bitcast.362), channel_id=1, source_target_pairs={{4,0},{8,4},{12,8},{16,12},{20,16},{24,20},{28,24},{0,28},{5,1},{9... | collective-permute-start | bytes 124808 | tf_op jit(solution)/shard_map/ppermute | solution.py:67
  57.3 2.1 %collective-permute-done.10 = f32[5,1,16,130]{3,2,0,1:T(8,128)S(1)} collective-permute-done((f32[5,1,16,130]{3,2,0,1:T(8,128)S(1)}, f32[5,1,16,130]{3,2,0,1:T(8,128)S(1)}, u32[]{:S(2)}, u32[]{:S(2)}) %collective-permute-start.10) | collective-permute-done | bytes 41632 | tf_op jit(solution)/shard_map/ppermute | solution.py:67
  62.6 0.9 %constant_dynamic-update-slice_fusion.33 = (f32[20,2,16,128]{3,2,1,0:T(8,128)S(1)}, f32[2,16,128]{2,1,0:T(8,128)S(1)}, f32[2,16,128]{2,1,0:T(8,128)S(1)}) fusion(f32[20,2,16,128]{3,2,1,0:T(8,128)S(1)} %get-tuple-element.32, pred[2,16,128]{2,1,0:T(8,128)(4,1)S(1)} %get-tuple-element.53, f32[4,16,130]{2,1,0:T(8,128)} %get-tuple-element.73, ...), kind=kLoop, calls=%fused_computation.74 | loop fusion | flops 262144 | bytes 505856
  64.6 1.3 %copy.156 = f32[20,2,16,128]{2,1,3,0:T(2,128)S(1)} copy(f32[20,2,16,128]{3,2,1,0:T(8,128)S(1)} %constant_dynamic-update-slice_fusion.15) | data formatting | bytes 655360 | tf_op jit(solution)/shard_map/concatenate | solution.py:184
  67.5 3.6 %collective-permute-start.13 = (f32[6,2,16,1]{2,1,0,3:T(2,128)S(1)}, f32[6,2,16,1]{2,1,0,3:T(2,128)S(1)}, u32[]{:S(2)}, u32[]{:S(2)}) collective-permute-start(f32[6,2,16,1]{2,1,0,3:T(2,128)S(1)} %bitcast.372), channel_id=1, source_target_pairs={{1,0},{2,1},{3,2},{0,3},{5,4},{6,5},{7,6},{4,7},{9,8},{10,9},{11,1... | collective-permute-start | bytes 2312 | tf_op jit(solution)/shard_map/ppermute | solution.py:67
  71.1 1.0 %collective-permute-done.12 = f32[6,2,16,1]{2,1,0,3:T(2,128)S(1)} collective-permute-done((f32[6,2,16,1]{2,1,0,3:T(2,128)S(1)}, f32[6,2,16,1]{2,1,0,3:T(2,128)S(1)}, u32[]{:S(2)}, u32[]{:S(2)}) %collective-permute-start.12) | collective-permute-done | bytes 800 | tf_op jit(solution)/shard_map/ppermute | solution.py:67
  75.7 2.9 %collective-permute-start.15 = (f32[6,1,16,130]{3,2,0,1:T(8,128)S(1)}, f32[6,1,16,130]{3,2,0,1:T(8,128)S(1)}, u32[]{:S(2)}, u32[]{:S(2)}) collective-permute-start(f32[6,1,16,130]{3,2,0,1:T(8,128)S(1)} %bitcast.350), channel_id=1, source_target_pairs={{4,0},{8,4},{12,8},{16,12},{20,16},{24,20},{28,24},{0,28},{5,1},{9... | collective-permute-start | bytes 149768 | tf_op jit(solution)/shard_map/ppermute | solution.py:67
  78.6 2.1 %collective-permute-done.14 = f32[6,1,16,130]{3,2,0,1:T(8,128)S(1)} collective-permute-done((f32[6,1,16,130]{3,2,0,1:T(8,128)S(1)}, f32[6,1,16,130]{3,2,0,1:T(8,128)S(1)}, u32[]{:S(2)}, u32[]{:S(2)}) %collective-permute-start.14) | collective-permute-done | bytes 49952 | tf_op jit(solution)/shard_map/ppermute | solution.py:67
  (414 shorter events, 39.1 us)
Async XLA Ops:
  0.7 9.9 %copy-start.85 = (s32[5]{0:T(128)S(1)}, s32[5]{0:T(128)}, u32[]{:S(2)}) copy-start(s32[5]{0:T(128)} %constant.411) | copy-start | bytes 64
  0.7 11.8 %copy-start.1 = (f32[15,2,16,128]{3,2,1,0:T(8,128)S(1)}, f32[15,2,16,128]{3,2,1,0:T(8,128)}, u32[]{:S(2)}) copy-start(f32[15,2,16,128]{3,2,1,0:T(8,128)} %param.35) | copy-start | bytes 737284
  3.1 9.6 %copy-start.11 = (s32[5]{0:T(128)S(1)}, s32[5]{0:T(128)}, u32[]{:S(2)}) copy-start(s32[5]{0:T(128)} %constant.439) | copy-start | bytes 64
  3.2 11.2 %copy-start.18 = (s32[5]{0:T(128)S(1)}, s32[5]{0:T(128)}, u32[]{:S(2)}) copy-start(s32[5]{0:T(128)} %constant.438) | copy-start | bytes 64
  3.8 6.7 %collective-permute-start = (f32[5,2,16,1]{2,1,0,3:T(2,128)S(1)}, f32[5,2,16,1]{2,1,0,3:T(2,128)S(1)}, u32[]{:S(2)}, u32[]{:S(2)}) collective-permute-start(f32[5,2,16,1]{2,1,0,3:T(2,128)S(1)} %bitcast.381), channel_id=1, source_target_pairs={{3,0},{0,1},{1,2},{2,3},{7,4},{4,5},{5,6},{6,7},{11,8},{8,9},{9,10... | collective-permute-start | bytes 1928 | tf_op jit(solution)/shard_map/ppermute | solution.py:67
  7.5 4.0 %collective-permute-start.1 = (f32[5,2,16,1]{2,1,0,3:T(2,128)S(1)}, f32[5,2,16,1]{2,1,0,3:T(2,128)S(1)}, u32[]{:S(2)}, u32[]{:S(2)}) collective-permute-start(f32[5,2,16,1]{2,1,0,3:T(2,128)S(1)} %bitcast.379), channel_id=1, source_target_pairs={{1,0},{2,1},{3,2},{0,3},{5,4},{6,5},{7,6},{4,7},{9,8},{10,9},{11,1... | collective-permute-start | bytes 1928 | tf_op jit(solution)/shard_map/ppermute | solution.py:67
  11.5 8.3 %copy-start.82 = (s32[5]{0:T(128)S(1)}, s32[5]{0:T(128)}, u32[]{:S(2)}) copy-start(s32[5]{0:T(128)} %constant.410) | copy-start | bytes 64
  13.3 3.1 %collective-permute-start.3 = (f32[5,1,16,130]{3,2,0,1:T(8,128)S(1)}, f32[5,1,16,130]{3,2,0,1:T(8,128)S(1)}, u32[]{:S(2)}, u32[]{:S(2)}) collective-permute-start(f32[5,1,16,130]{3,2,0,1:T(8,128)S(1)} %bitcast.365), channel_id=1, source_target_pairs={{4,0},{8,4},{12,8},{16,12},{20,16},{24,20},{28,24},{0,28},{5,1},{9... | collective-permute-start | bytes 124808 | tf_op jit(solution)/shard_map/ppermute | solution.py:67
  15.0 4.8 %collective-permute-start.2 = (f32[5,1,16,130]{3,2,0,1:T(8,128)S(1)}, f32[5,1,16,130]{3,2,0,1:T(8,128)S(1)}, u32[]{:S(2)}, u32[]{:S(2)}) collective-permute-start(f32[5,1,16,130]{3,2,0,1:T(8,128)S(1)} %bitcast.363), channel_id=1, source_target_pairs={{28,0},{0,4},{4,8},{8,12},{12,16},{16,20},{20,24},{24,28},{29,1},{... | collective-permute-start | bytes 124808 | tf_op jit(solution)/shard_map/ppermute | solution.py:67
  23.9 8.6 %copy-start.8 = (s32[6]{0:T(128)S(1)}, s32[6]{0:T(128)}, u32[]{:S(2)}) copy-start(s32[6]{0:T(128)} %constant.475) | copy-start | bytes 76
  24.5 5.5 %collective-permute-start.4 = (f32[6,2,16,1]{2,1,0,3:T(2,128)S(1)}, f32[6,2,16,1]{2,1,0,3:T(2,128)S(1)}, u32[]{:S(2)}, u32[]{:S(2)}) collective-permute-start(f32[6,2,16,1]{2,1,0,3:T(2,128)S(1)} %bitcast.377), channel_id=1, source_target_pairs={{3,0},{0,1},{1,2},{2,3},{7,4},{4,5},{5,6},{6,7},{11,8},{8,9},{9,10... | collective-permute-start | bytes 2312 | tf_op jit(solution)/shard_map/ppermute | solution.py:67
  25.9 5.3 %collective-permute-start.5 = (f32[6,2,16,1]{2,1,0,3:T(2,128)S(1)}, f32[6,2,16,1]{2,1,0,3:T(2,128)S(1)}, u32[]{:S(2)}, u32[]{:S(2)}) collective-permute-start(f32[6,2,16,1]{2,1,0,3:T(2,128)S(1)} %bitcast.373), channel_id=1, source_target_pairs={{1,0},{2,1},{3,2},{0,3},{5,4},{6,5},{7,6},{4,7},{9,8},{10,9},{11,1... | collective-permute-start | bytes 2312 | tf_op jit(solution)/shard_map/ppermute | solution.py:67
  33.1 2.8 %collective-permute-start.7 = (f32[6,1,16,130]{3,2,0,1:T(8,128)S(1)}, f32[6,1,16,130]{3,2,0,1:T(8,128)S(1)}, u32[]{:S(2)}, u32[]{:S(2)}) collective-permute-start(f32[6,1,16,130]{3,2,0,1:T(8,128)S(1)} %bitcast.353), channel_id=1, source_target_pairs={{4,0},{8,4},{12,8},{16,12},{20,16},{24,20},{28,24},{0,28},{5,1},{9... | collective-permute-start | bytes 149768 | tf_op jit(solution)/shard_map/ppermute | solution.py:67
  33.8 5.0 %collective-permute-start.6 = (f32[6,1,16,130]{3,2,0,1:T(8,128)S(1)}, f32[6,1,16,130]{3,2,0,1:T(8,128)S(1)}, u32[]{:S(2)}, u32[]{:S(2)}) collective-permute-start(f32[6,1,16,130]{3,2,0,1:T(8,128)S(1)} %bitcast.351), channel_id=1, source_target_pairs={{28,0},{0,4},{4,8},{8,12},{12,16},{16,20},{20,24},{24,28},{29,1},{... | collective-permute-start | bytes 149768 | tf_op jit(solution)/shard_map/ppermute | solution.py:67
  45.1 14.3 %copy-start.83 = (s32[5]{0:T(128)S(1)}, s32[5]{0:T(128)}, u32[]{:S(2)}) copy-start(s32[5]{0:T(128)} %constant.410) | copy-start | bytes 64
  45.7 5.5 %collective-permute-start.8 = (f32[5,2,16,1]{2,1,0,3:T(2,128)S(1)}, f32[5,2,16,1]{2,1,0,3:T(2,128)S(1)}, u32[]{:S(2)}, u32[]{:S(2)}) collective-permute-start(f32[5,2,16,1]{2,1,0,3:T(2,128)S(1)} %bitcast.380), channel_id=1, source_target_pairs={{3,0},{0,1},{1,2},{2,3},{7,4},{4,5},{5,6},{6,7},{11,8},{8,9},{9,10... | collective-permute-start | bytes 1928 | tf_op jit(solution)/shard_map/ppermute | solution.py:67
  46.4 5.8 %collective-permute-start.9 = (f32[5,2,16,1]{2,1,0,3:T(2,128)S(1)}, f32[5,2,16,1]{2,1,0,3:T(2,128)S(1)}, u32[]{:S(2)}, u32[]{:S(2)}) collective-permute-start(f32[5,2,16,1]{2,1,0,3:T(2,128)S(1)} %bitcast.378), channel_id=1, source_target_pairs={{1,0},{2,1},{3,2},{0,3},{5,4},{6,5},{7,6},{4,7},{9,8},{10,9},{11,1... | collective-permute-start | bytes 1928 | tf_op jit(solution)/shard_map/ppermute | solution.py:67
  54.0 5.4 %collective-permute-start.10 = (f32[5,1,16,130]{3,2,0,1:T(8,128)S(1)}, f32[5,1,16,130]{3,2,0,1:T(8,128)S(1)}, u32[]{:S(2)}, u32[]{:S(2)}) collective-permute-start(f32[5,1,16,130]{3,2,0,1:T(8,128)S(1)} %bitcast.364), channel_id=1, source_target_pairs={{28,0},{0,4},{4,8},{8,12},{12,16},{16,20},{20,24},{24,28},{29,1},{... | collective-permute-start | bytes 124808 | tf_op jit(solution)/shard_map/ppermute | solution.py:67
  54.6 5.5 %collective-permute-start.11 = (f32[5,1,16,130]{3,2,0,1:T(8,128)S(1)}, f32[5,1,16,130]{3,2,0,1:T(8,128)S(1)}, u32[]{:S(2)}, u32[]{:S(2)}) collective-permute-start(f32[5,1,16,130]{3,2,0,1:T(8,128)S(1)} %bitcast.362), channel_id=1, source_target_pairs={{4,0},{8,4},{12,8},{16,12},{20,16},{24,20},{28,24},{0,28},{5,1},{9... | collective-permute-start | bytes 124808 | tf_op jit(solution)/shard_map/ppermute | solution.py:67
  64.6 7.5 %copy-start.84 = (s32[6]{0:T(128)S(1)}, s32[6]{0:T(128)}, u32[]{:S(2)}) copy-start(s32[6]{0:T(128)} %constant.449) | copy-start | bytes 76
  66.5 5.5 %collective-permute-start.12 = (f32[6,2,16,1]{2,1,0,3:T(2,128)S(1)}, f32[6,2,16,1]{2,1,0,3:T(2,128)S(1)}, u32[]{:S(2)}, u32[]{:S(2)}) collective-permute-start(f32[6,2,16,1]{2,1,0,3:T(2,128)S(1)} %bitcast.376), channel_id=1, source_target_pairs={{3,0},{0,1},{1,2},{2,3},{7,4},{4,5},{5,6},{6,7},{11,8},{8,9},{9,10... | collective-permute-start | bytes 2312 | tf_op jit(solution)/shard_map/ppermute | solution.py:67
  67.5 5.6 %collective-permute-start.13 = (f32[6,2,16,1]{2,1,0,3:T(2,128)S(1)}, f32[6,2,16,1]{2,1,0,3:T(2,128)S(1)}, u32[]{:S(2)}, u32[]{:S(2)}) collective-permute-start(f32[6,2,16,1]{2,1,0,3:T(2,128)S(1)} %bitcast.372), channel_id=1, source_target_pairs={{1,0},{2,1},{3,2},{0,3},{5,4},{6,5},{7,6},{4,7},{9,8},{10,9},{11,1... | collective-permute-start | bytes 2312 | tf_op jit(solution)/shard_map/ppermute | solution.py:67
  75.1 5.6 %collective-permute-start.14 = (f32[6,1,16,130]{3,2,0,1:T(8,128)S(1)}, f32[6,1,16,130]{3,2,0,1:T(8,128)S(1)}, u32[]{:S(2)}, u32[]{:S(2)}) collective-permute-start(f32[6,1,16,130]{3,2,0,1:T(8,128)S(1)} %bitcast.352), channel_id=1, source_target_pairs={{28,0},{0,4},{4,8},{8,12},{12,16},{16,20},{20,24},{24,28},{29,1},{... | collective-permute-start | bytes 149768 | tf_op jit(solution)/shard_map/ppermute | solution.py:67
  75.7 5.7 %collective-permute-start.15 = (f32[6,1,16,130]{3,2,0,1:T(8,128)S(1)}, f32[6,1,16,130]{3,2,0,1:T(8,128)S(1)}, u32[]{:S(2)}, u32[]{:S(2)}) collective-permute-start(f32[6,1,16,130]{3,2,0,1:T(8,128)S(1)} %bitcast.350), channel_id=1, source_target_pairs={{4,0},{8,4},{12,8},{16,12},{20,16},{24,20},{28,24},{0,28},{5,1},{9... | collective-permute-start | bytes 149768 | tf_op jit(solution)/shard_map/ppermute | solution.py:67
  (81 other events, 156.1 us)
where the time goes:
time: 88 us; the launch traced here: 87.6 us
  local copies, waits for them, and re-layouts  36.4 us (41%)
  starting transfers between devices  24.3 us (28%)
  waiting for transfers between devices  15.7 us (18%)
  other arithmetic  8.74 us (10%)
  between operations  2.45 us (3%)
    ppermute x16, starting transfers between devices, shifted(): return lax.ppermute(block, axis, route)  24.3 us
    ppermute x16, waiting for transfers between devices, shifted(): return lax.ppermute(block, axis, route)  15.7 us
    unnamed x64, other arithmetic  6.14 us
    slice x84, local copies, waits for them, and re-layouts, pull_plane(): return jnp.roll(window, vector[2], axis=1)  4.53 us
    scatter x8, local copies, waits for them, and re-layouts, with_rims(): left_column = empty_column.at[jnp.array(upward_rows)].set(upper)  4.08 us
    scatter x8, local copies, waits for them, and re-layouts, with_rims(): right_column = empty_column.at[jnp.array(downward_rows)].set(lower)  3.95 us
    unnamed x179, local copies, waits for them, and re-layouts  3.93 us
    scatter x4, local copies, waits for them, and re-layouts, place_layers(): right_layer = empty_layer.at[jnp.array(backward_rows)].set(behind)  2.85 us
  transfers between devices with their start and end apart: 16, of which 10 were waited for; matrix products, arithmetic and copies ran while one was open for 13% of the time, Pallas kernels for 0%

commit v1 on v0

v1 whole, which is shorter than its diff:
```python
import functools

import jax
import jax.numpy as jnp
from jax import lax
from jax.experimental import pallas as pl
from jax.experimental.pallas import tpu as pltpu
from jax.sharding import PartitionSpec as P

STEPS = 2
PHASE_VELOCITIES = [
    (0, 0, 0), (1, 0, 0), (-1, 0, 0), (0, 1, 0), (0, -1, 0), (0, 0, 1), (0, 0, -1),
    (1, 1, 1), (1, 1, -1), (1, -1, 1), (1, -1, -1),
    (-1, 1, 1), (-1, 1, -1), (-1, -1, 1), (-1, -1, -1),
]
PHASE_WEIGHTS = [2.0 / 9.0] + [1.0 / 9.0] * 6 + [1.0 / 72.0] * 8
FLOW_VELOCITIES = [
    (0, 0, 0), (1, 0, 0), (-1, 0, 0), (0, 1, 0), (0, -1, 0), (0, 0, 1), (0, 0, -1),
    (1, 1, 0), (1, -1, 0), (-1, 1, 0), (-1, -1, 0),
    (1, 0, 1), (1, 0, -1), (-1, 0, 1), (-1, 0, -1),
    (0, 1, 1), (0, 1, -1), (0, -1, 1), (0, -1, -1),
]
FLOW_WEIGHTS = [1.0 / 3.0] + [1.0 / 18.0] * 6 + [1.0 / 36.0] * 12
SURFACE_TENSION = 0.05
INTERFACE_WIDTH = 4.0
GRADIENT_FLOOR = 0.1
PHASE_LAMBDA = 0.3
PHASE_RELAX = 0.8
BETA = 12.0 * SURFACE_TENSION / INTERFACE_WIDTH
KAPPA = 1.5 * SURFACE_TENSION * INTERFACE_WIDTH

MESH = pl.DeviceIdType.MESH
SIDES = [(-1, 0), (1, 0), (0, -1), (0, 1), (-1, -1), (-1, 1), (1, -1), (1, 1)]


def moving(velocities, coordinate, sign):
    return [n for n, vector in enumerate(velocities) if vector[coordinate] == sign]


CROSSING = {
    sign: [("h", n) for n in moving(PHASE_VELOCITIES, 0, sign)]
    + [("f", n) for n in moving(FLOW_VELOCITIES, 0, sign)]
    for sign in (1, -1)
}


def opposite(velocities, n):
    vector = velocities[n]
    return velocities.index((-vector[0], -vector[1], -vector[2]))


def slot_table(nx):
    slots = {}
    for sign in (1, -1):
        for kind, velocities in (("h", PHASE_VELOCITIES), ("f", FLOW_VELOCITIES)):
            for n in moving(velocities, 1, sign):
                for x in range(nx):
                    slots[kind, n, x] = len(slots)
    for kind in ("edge+", "edge-", "push+", "push-"):
        for x in range(-1, nx + 1):
            slots[kind, x] = len(slots)
    return slots


def kernel(
    size_gx, size_gy, phase_in, flow_in, solid_in, phase_out, flow_out,
    h_buf, f_buf, solid, slab_out, slab_in, pack_out, pack_in,
    load_sem, store_sem, slab_send, slab_recv, pack_send, pack_recv,
):
    nx, nz, ny = solid.shape
    slots = slot_table(nx)
    assert len(slots) <= ny
    gx, gy = lax.axis_index("gx"), lax.axis_index("gy")

    def device(side):
        return (lax.rem(gx + side[0] + size_gx, size_gx), lax.rem(gy + side[1] + size_gy, size_gy))

    loads = [
        pltpu.make_async_copy(phase_in, h_buf.at[0], load_sem.at[0]),
        pltpu.make_async_copy(flow_in, f_buf.at[0], load_sem.at[1]),
        pltpu.make_async_copy(solid_in, solid, load_sem.at[2]),
    ]
    for load in loads:
        load.start()
    barrier = pltpu.get_barrier_semaphore()
    for side in SIDES:
        pl.semaphore_signal(barrier, inc=1, device_id=device(side), device_id_type=MESH)

    lanes = lax.broadcasted_iota(jnp.int32, (nz, ny), 1)
    first, last = lanes == 0, lanes == ny - 1

    def turn(tile, shift, axis):
        shift %= tile.shape[axis]
        return pltpu.roll(tile, shift, axis) if shift else tile

    def up(tile):
        return turn(tile, -1, 0)

    def down(tile):
        return turn(tile, 1, 0)

    def pushes(step):
        grouped = {}
        for x in range(nx):
            for n, (cx, cy, cz) in enumerate(PHASE_VELOCITIES):
                value = turn(h_buf[step, n, x], cz, 0)
                key = (cy, x + cx)
                grouped[key] = grouped[key] + value if key in grouped else value
        inside = {}
        for x in range(-1, nx + 1):
            inside[x] = (
                grouped[0, x]
                + jnp.where(first, 0.0, turn(grouped[1, x], 1, 1))
                + jnp.where(last, 0.0, turn(grouped[-1, x], -1, 1))
            )
        packed = jnp.zeros((nz, ny), jnp.float32)
        for key, slot in slots.items():
            if key[0] in ("h", "f"):
                kind, n, x = key
                velocities, buf = (PHASE_VELOCITIES, h_buf) if kind == "h" else (FLOW_VELOCITIES, f_buf)
                sign, tile = velocities[n][1], buf[step, n, x]
            else:
                sign = 1 if key[0][-1] == "+" else -1
                tile = inside[key[1]] if key[0][:4] == "edge" else grouped[sign, key[1]]
            source = ny - 1 if sign == 1 else 0
            packed = jnp.where(lanes == slot, turn(tile, slot - source, 1), packed)
        pack_out[step, 0] = inside[0]
        pack_out[step, 1] = packed
        pack_out[step, 2] = inside[nx - 1]
        return grouped, inside, packed

    def fill_slab(step):
        for place, sign in enumerate((-1, 1)):
            x = 0 if sign == -1 else nx - 1
            for k, (kind, n) in enumerate(CROSSING[sign]):
                slab_out[step, place, k] = (h_buf if kind == "h" else f_buf)[step, n, x]

    def slab_copies(step):
        return [
            pltpu.make_async_remote_copy(
                slab_out.at[step, place], slab_in.at[step, place],
                slab_send.at[step, place], slab_recv.at[step, place],
                device_id=device(SIDES[place]), device_id_type=MESH,
            )
            for place in range(2)
        ]

    def pack_copies(step):
        copies = []
        for place, side in enumerate(SIDES):
            begin, length = (0, 2) if place == 0 else (1, 2) if place == 1 else (1, 1)
            copies.append(
                pltpu.make_async_remote_copy(
                    pack_out.at[step, pl.ds(begin, length)],
                    pack_in.at[step, place, pl.ds(0, length)],
                    pack_send.at[step, place], pack_recv.at[step, place],
                    device_id=device(side), device_id_type=MESH,
                )
            )
        return copies

    def collide(step, own, store):
        grouped, inside, packed = own

        def from_side(side):
            if side == (0, 0):
                return packed
            place = SIDES.index((-side[0], -side[1]))
            return pack_in[step, place, 1 if place == 0 else 0]

        def pulled(kind, n, x):
            velocities, buf = (PHASE_VELOCITIES, h_buf) if kind == "h" else (FLOW_VELOCITIES, f_buf)
            cx, cy, cz = velocities[n]
            source = x - cx
            side = -1 if source < 0 else 1 if source >= nx else 0
            if side == 0:
                tile = buf[step, n, source]
            else:
                tile = slab_in[step, 0 if side == 1 else 1, CROSSING[-side].index((kind, n))]
            if cy:
                column = from_side((side, -cy))
                slot = slots[kind, n, source - side * nx]
                edge = 0 if cy == 1 else ny - 1
                tile = jnp.where(lanes == edge, turn(column, edge - slot, 1), turn(tile, cy, 1))
            return turn(tile, cz, 0)

        phase_read = [[pulled("h", n, x) for n in range(15)] for x in range(nx)]
        field = {x: functools.reduce(jnp.add, phase_read[x]) for x in range(nx)}

        def column_sum(kind, x, gy_side):
            total = None
            for side in (0, 1, -1):
                at = x - side * nx
                if -1 <= at <= nx:
                    value = turn(from_side((side, gy_side)), -slots[kind, at], 1)
                    total = value if total is None else total + value
            return total

        for x, edge_layer, side in ((-1, nx - 1, -1), (nx, 0, 1)):
            place = SIDES.index((-side, 0))
            value = inside[x] + pack_in[step, place, 0 if place == 0 else 1]
            for kind, gy_side, where in (("push+", -1, 0), ("push-", 1, ny - 1)):
                added = None
                for across in (0, side):
                    at = x - across * nx
                    term = turn(from_side((across, gy_side)), where - slots[kind, at], 1)
                    added = term if added is None else added + term
                value = value + jnp.where(lanes == where, added, 0.0)
            field[x] = value

        flat, sideways, steep, deep = {}, {}, {}, {}
        star = {}
        for x in range(-1, nx + 1):
            phi = field[x]
            before = column_sum("push-", x, 0) + column_sum("edge+", x, -1)
            after = turn(column_sum("push+", x, 0) + column_sum("edge-", x, 1), ny - 1, 1)
            left = jnp.where(first, before, turn(phi, 1, 1))
            right = jnp.where(last, after, turn(phi, -1, 1))
            above, below = up(phi), down(phi)
            flat[x] = left + right
            sideways[x] = right - left
            steep[x] = above - below
            deep[x] = above + below
            star[x] = 2.0 * phi + flat[x] + deep[x]

        for x in range(nx):
            phi = field[x]
            dy, ys = sideways[x], flat[x]
            ys_up, ys_down = up(ys), down(ys)
            dx_grad = (star[x + 1] - star[x - 1]) * (1.0 / 12.0)
            dy_grad = (2.0 * dy + sideways[x + 1] + sideways[x - 1] + up(dy) + down(dy)) * (1.0 / 12.0)
            dz_grad = (2.0 * steep[x] + steep[x + 1] + steep[x - 1] + ys_up - ys_down) * (1.0 / 12.0)
            ringed = star[x + 1] + star[x - 1] + 2.0 * (ys + deep[x]) + ys_up + ys_down
            laplacian = ringed * (1.0 / 6.0) - 4.0 * phi
            gradient = (dx_grad, dy_grad, dz_grad)
            squared = dx_grad * dx_grad + dy_grad * dy_grad + dz_grad * dz_grad
            scaling = lax.rsqrt(jnp.maximum(squared, GRADIENT_FLOOR * GRADIENT_FLOOR))
            clipped = jnp.clip(phi, 0.0, 1.0)
            inv_density = 1.0 / (1.0 + 2.0 * clipped)
            inv_time = 1.0 / (0.6 + 0.4 * clipped)
            potential = 4.0 * BETA * phi * (phi - 1.0) * (phi - 0.5) - KAPPA * laplacian
            force = [potential * component for component in gradient]
            read = [pulled("f", n, x) for n in range(19)]
            pressure = functools.reduce(jnp.add, read)
            velocity = []
            for coordinate in range(3):
                moment = 0.5 * force[coordinate]
                for n in range(19):
                    if FLOW_VELOCITIES[n][coordinate] == 1:
                        moment = moment + read[n]
                    elif FLOW_VELOCITIES[n][coordinate] == -1:
                        moment = moment - read[n]
                velocity.append(moment * inv_density)
            speed_sq = velocity[0] * velocity[0] + velocity[1] * velocity[1] + velocity[2] * velocity[2]
            force_factor = 3.0 * (1.0 - 0.5 * inv_time) * inv_density
            keep = 1.0 - inv_time
            drift = [3.0 * inv_time * velocity[k] + force_factor * force[k] for k in range(3)]
            level = inv_time * (pressure - 1.5 * speed_sq)
            curve = 4.5 * inv_time
            solid_cells = solid[x] > 0

            def along(vector, values):
                total = None
                for c, value in zip(vector, values):
                    if c == 0:
                        continue
                    if total is None:
                        total = value
                        assert c == 1
                    else:
                        total = total + value if c == 1 else total - value
                return total

            store("f", 0, x, jnp.where(solid_cells, read[0], read[0] * keep + FLOW_WEIGHTS[0] * level))
            for weight in sorted(set(FLOW_WEIGHTS[1:])):
                level_w, curve_w = weight * level, weight * curve
                drift_w = [weight * value for value in drift]
                for n in range(1, 19):
                    vector = FLOW_VELOCITIES[n]
                    if FLOW_WEIGHTS[n] != weight or [c for c in vector if c][0] != 1:
                        continue
                    m = opposite(FLOW_VELOCITIES, n)
                    speed = along(vector, velocity)
                    even = level_w + curve_w * (speed * speed)
                    odd = along(vector, drift_w)
                    store("f", n, x, jnp.where(solid_cells, read[m], read[n] * keep + (even + odd)))
                    store("f", m, x, jnp.where(solid_cells, read[n], read[m] * keep + (even - odd)))

            gain = 1.0 / PHASE_RELAX
            interface = PHASE_LAMBDA * phi * (1.0 - phi) * scaling
            tilt = [3.0 * phi * velocity[k] + interface * gradient[k] for k in range(3)]
            pops = phase_read[x]
            store("h", 0, x, jnp.where(solid_cells, pops[0], (1.0 - gain) * pops[0] + gain * PHASE_WEIGHTS[0] * phi))
            for weight in sorted(set(PHASE_WEIGHTS[1:])):
                phi_w = (gain * weight) * phi
                tilt_w = [(gain * weight) * value for value in tilt]
                for n in range(1, 15):
                    vector = PHASE_VELOCITIES[n]
                    if PHASE_WEIGHTS[n] != weight or [c for c in vector if c][0] != 1:
                        continue
                    m = opposite(PHASE_VELOCITIES, n)
                    odd = along(vector, tilt_w)
                    store("h", n, x, jnp.where(solid_cells, pops[m], (1.0 - gain) * pops[n] + (phi_w + odd)))
                    store("h", m, x, jnp.where(solid_cells, pops[n], (1.0 - gain) * pops[m] + (phi_w - odd)))

    for load in loads:
        load.wait()
    started = []
    for step in range(STEPS):
        fill_slab(step)
        if step == 0:
            own = pushes(step)
            pl.semaphore_wait(barrier, len(SIDES))
            packs, slabs = pack_copies(step), slab_copies(step)
            for copy in packs + slabs:
                copy.start()
        else:
            slabs = slab_copies(step)
            for copy in slabs:
                copy.start()
            own = pushes(step)
            packs = pack_copies(step)
            for copy in packs:
                copy.start()
        started += packs + slabs
        for copy in packs + slabs:
            copy.wait_recv()

        def store(kind, n, x, value):
            (h_buf if kind == "h" else f_buf)[step + 1, n, x] = value

        collide(step, own, store)
    stores = [
        pltpu.make_async_copy(h_buf.at[STEPS], phase_out, store_sem.at[0]),
        pltpu.make_async_copy(f_buf.at[STEPS], flow_out, store_sem.at[1]),
    ]
    for copy in stores:
        copy.start()
    for copy in started:
        copy.wait_send()
    for copy in stores:
        copy.wait()


def shards(size_gx, size_gy, phase_pops, flow_pops, solid_flags):
    nx, nz, ny = solid_flags.shape
    f32 = jnp.float32
    crossing = len(CROSSING[1])
    anywhere = pl.BlockSpec(memory_space=pl.ANY)
    return pl.pallas_call(
        functools.partial(kernel, size_gx, size_gy),
        out_shape=(
            jax.ShapeDtypeStruct(phase_pops.shape, f32),
            jax.ShapeDtypeStruct(flow_pops.shape, f32),
        ),
        in_specs=[anywhere] * 3,
        out_specs=(anywhere, anywhere),
        scratch_shapes=[
            pltpu.VMEM((STEPS + 1,) + phase_pops.shape, f32),
            pltpu.VMEM((STEPS + 1,) + flow_pops.shape, f32),
            pltpu.VMEM((nx, nz, ny), jnp.int32),
            pltpu.VMEM((STEPS, 2, crossing, nz, ny), f32),
            pltpu.VMEM((STEPS, 2, crossing, nz, ny), f32),
            pltpu.VMEM((STEPS, 3, nz, ny), f32),
            pltpu.VMEM((STEPS, len(SIDES), 2, nz, ny), f32),
            pltpu.SemaphoreType.DMA((3,)),
            pltpu.SemaphoreType.DMA((2,)),
            pltpu.SemaphoreType.DMA((STEPS, 2)),
            pltpu.SemaphoreType.DMA((STEPS, 2)),
            pltpu.SemaphoreType.DMA((STEPS, len(SIDES))),
            pltpu.SemaphoreType.DMA((STEPS, len(SIDES))),
        ],
        compiler_params=pltpu.CompilerParams(collective_id=0, has_side_effects=True),
    )(phase_pops, flow_pops, solid_flags)


def solution(mesh):
    placed = P(None, "gx", None, "gy")
    return jax.shard_map(
        functools.partial(shards, mesh.shape["gx"], mesh.shape["gy"]),
        mesh=mesh,
        in_specs=(placed, placed, P("gx", None, "gy")),
        out_specs=(placed, placed),
        check_vma=False,
    )
```

time: 88 us -> 21.2 us (0.24)
  local copies, waits for them, and re-layouts: 36.4 us -> 2.42 us
  starting transfers between devices: 24.3 us -> 0 us
  Pallas kernels: 0 us -> 17.9 us
  waiting for transfers between devices: 15.7 us -> 0 us
  other arithmetic: 8.74 us -> 0 us
  between operations: 2.45 us -> 0.65 us
    ppermute x16 -> x0, starting transfers between devices: 24.3 us -> none  [shifted(): return lax.ppermute(block, axis, route)]
    pallas_call x0 -> x1, Pallas kernels: none -> 17.9 us  [shards(): pl.pallas_call(functools.partial(kernel, size_gx, size_gy), out_shape=(ja...]
    ppermute x16 -> x0, waiting for transfers between devices: 15.7 us -> none  [shifted(): return lax.ppermute(block, axis, route)]
    scatter x24 -> x0, local copies, waits for them, and re-layouts: 13.7 us -> none  [the longest x8 4.08 us: with_rims(): left_column = empty_column.at[jnp.array(upward_rows)].set(upper)]
    gather x16 -> x0, local copies, waits for them, and re-layouts: 9.45 us -> none  [the longest x4 2.42 us: with_rims(): upper = shifted(stacked[jnp.array(upward_rows), :, :, -1:], 'gy', 1)]
    unnamed x64 -> x0, other arithmetic: 6.14 us -> none
    slice x84 -> x0, local copies, waits for them, and re-layouts: 4.53 us -> none  [pull_plane(): return jnp.roll(window, vector[2], axis=1)]
    concatenate x2 -> x0, local copies, waits for them, and re-layouts: 2.57 us -> none  [shards(): jnp.concatenate([phase_field[None], flow_pops], axis=0)]
  transfers between devices with their start and end apart: 16 -> 0, of which waited for: 10 -> 0; matrix products, arithmetic and copies ran while one was open for 13% -> 0% of each run, Pallas kernels for 0% -> 0%
where the time goes in v1:
time: 21.2 us; the launch traced here: 21 us
  Pallas kernels  17.9 us (84%)
  local copies, waits for them, and re-layouts  2.42 us (11%)
  between operations  0.65 us (3%)
    pallas_call x1, Pallas kernels, shards(): pl.pallas_call(functools.partial(kernel, size_gx, size_gy), out_shape=(ja...  17.9 us
    unnamed x4, local copies, waits for them, and re-layouts  2.42 us

profile of v1, /device:TPU:0, one launch (start us, length us, event | category | flops | bytes accessed | tf_op | source)
XLA Modules:
  0.0 21.0 jit_solution(11419416761662539001)
XLA Ops:
  0.6 17.9 %shard_map.50 = (f32[15,2,16,128]{3,2,1,0:T(8,128)}, f32[19,2,16,128]{3,2,1,0:T(8,128)}) custom-call(f32[15,2,16,128]{3,2,1,0:T(8,128)} %phase_in.1, f32[19,2,16,128]{3,2,1,0:T(8,128)} %flow_in.1, s32[2,16,128]{2,1,0:T(8,128)} %solid_in.1), custom_call_target="tpu_custom_call" | custom-call | tf_op jit(solution)/shard_map/pallas_call | solution.py:350
  18.6 0.0 copy-start
  18.6 1.7 %copy.7 = f32[15,2,16,128]{3,2,1,0:T(8,128)} copy(f32[15,2,16,128]{3,2,1,0:T(8,128)} %get-tuple-element.4) | data formatting | bytes 491520
  20.3 0.0 copy-done
  20.3 0.7 %copy.8 = f32[19,2,16,128]{3,2,1,0:T(8,128)} copy(f32[19,2,16,128]{3,2,1,0:T(8,128)S(1)} %copy-done) | data formatting | bytes 622592
Async XLA Ops:
  18.6 1.7 %copy-start = (f32[19,2,16,128]{3,2,1,0:T(8,128)S(1)}, f32[19,2,16,128]{3,2,1,0:T(8,128)}, u32[]{:S(2)}) copy-start(f32[19,2,16,128]{3,2,1,0:T(8,128)} %get-tuple-element.5) | copy-start | bytes 933892

commit v2 on v1

--- a/solution.py
+++ b/solution.py
@@ -65,7 +65,7 @@
 def kernel(
     size_gx, size_gy, phase_in, flow_in, solid_in, phase_out, flow_out,
     h_buf, f_buf, solid, slab_out, slab_in, pack_out, pack_in,
-    load_sem, store_sem, slab_send, slab_recv, pack_send, pack_recv,
+    load_sem, slab_send, slab_recv, pack_send, pack_recv,
 ):
     nx, nz, ny = solid.shape
     slots = slot_table(nx)
@@ -327,18 +327,24 @@
             copy.wait_recv()
 
         def store(kind, n, x, value):
-            (h_buf if kind == "h" else f_buf)[step + 1, n, x] = value
+            if step + 1 == STEPS:
+                (phase_out if kind == "h" else flow_out)[n, x] = value
+            else:
+                (h_buf if kind == "h" else f_buf)[step + 1, n, x] = value
 
         collide(step, own, store)
-    stores = [
-        pltpu.make_async_copy(h_buf.at[STEPS], phase_out, store_sem.at[0]),
-        pltpu.make_async_copy(f_buf.at[STEPS], flow_out, store_sem.at[1]),
-    ]
-    for copy in stores:
-        copy.start()
     for copy in started:
         copy.wait_send()
-    for copy in stores:
+
+
+def write_back(phase, flow, phase_out, flow_out, sems):
+    copies = [
+        pltpu.make_async_copy(phase, phase_out, sems.at[0]),
+        pltpu.make_async_copy(flow, flow_out, sems.at[1]),
+    ]
+    for copy in copies:
+        copy.start()
+    for copy in copies:
         copy.wait()
 
 
@@ -347,24 +353,22 @@
     f32 = jnp.float32
     crossing = len(CROSSING[1])
     anywhere = pl.BlockSpec(memory_space=pl.ANY)
-    return pl.pallas_call(
+    shapes = (phase_pops.shape, flow_pops.shape)
+    on_chip = pl.BlockSpec(memory_space=pltpu.VMEM)
+    results = pl.pallas_call(
         functools.partial(kernel, size_gx, size_gy),
-        out_shape=(
-            jax.ShapeDtypeStruct(phase_pops.shape, f32),
-            jax.ShapeDtypeStruct(flow_pops.shape, f32),
-        ),
+        out_shape=tuple(pltpu.VMEM(shape, f32) for shape in shapes),
         in_specs=[anywhere] * 3,
-        out_specs=(anywhere, anywhere),
+        out_specs=(on_chip, on_chip),
         scratch_shapes=[
-            pltpu.VMEM((STEPS + 1,) + phase_pops.shape, f32),
-            pltpu.VMEM((STEPS + 1,) + flow_pops.shape, f32),
+            pltpu.VMEM((STEPS,) + phase_pops.shape, f32),
+            pltpu.VMEM((STEPS,) + flow_pops.shape, f32),
             pltpu.VMEM((nx, nz, ny), jnp.int32),
             pltpu.VMEM((STEPS, 2, crossing, nz, ny), f32),
             pltpu.VMEM((STEPS, 2, crossing, nz, ny), f32),
             pltpu.VMEM((STEPS, 3, nz, ny), f32),
             pltpu.VMEM((STEPS, len(SIDES), 2, nz, ny), f32),
             pltpu.SemaphoreType.DMA((3,)),
-            pltpu.SemaphoreType.DMA((2,)),
             pltpu.SemaphoreType.DMA((STEPS, 2)),
             pltpu.SemaphoreType.DMA((STEPS, 2)),
             pltpu.SemaphoreType.DMA((STEPS, len(SIDES))),
@@ -372,6 +376,13 @@
         ],
         compiler_params=pltpu.CompilerParams(collective_id=0, has_side_effects=True),
     )(phase_pops, flow_pops, solid_flags)
+    return pl.pallas_call(
+        write_back,
+        out_shape=tuple(jax.ShapeDtypeStruct(shape, f32) for shape in shapes),
+        in_specs=[on_chip, on_chip],
+        out_specs=(anywhere, anywhere),
+        scratch_shapes=[pltpu.SemaphoreType.DMA((2,))],
+    )(*[pltpu.with_memory_space_constraint(r, pltpu.VMEM) for r in results])
 
 
 def solution(mesh):

time: 21.2 us -> 18.8 us (0.89)
  local copies, waits for them, and re-layouts: 2.42 us -> 0 us
    unnamed x4 -> x0, local copies, waits for them, and re-layouts: 2.42 us -> none
    pallas_call x1 -> x2, Pallas kernels: 17.9 us -> 18 us  [the longest x1 17.2 us: shards(): pl.pallas_call(functools.partial(kernel, size_gx, size_gy), out_shape=tup...]
where the time goes in v2:
time: 18.8 us; the launch traced here: 18.6 us
  Pallas kernels  18 us (96%)
  between operations  0.64 us (3%)
    pallas_call x1, Pallas kernels, shards(): pl.pallas_call(functools.partial(kernel, size_gx, size_gy), out_shape=tup...  17.2 us
    pallas_call x1, Pallas kernels, shards(): pl.pallas_call(write_back, out_shape=tuple((jax.ShapeDtypeStruct(shape, f...  0.82 us

profile of v2, /device:TPU:0, one launch (start us, length us, event | category | flops | bytes accessed | tf_op | source)
XLA Modules:
  0.0 18.6 jit_solution(12786006513643949236)
XLA Ops:
  0.6 17.2 %shard_map.50 = (f32[15,2,16,128]{3,2,1,0:T(8,128)S(1)}, f32[19,2,16,128]{3,2,1,0:T(8,128)S(1)}) custom-call(f32[15,2,16,128]{3,2,1,0:T(8,128)} %phase_in.1, f32[19,2,16,128]{3,2,1,0:T(8,128)} %flow_in.1, s32[2,16,128]{2,1,0:T(8,128)} %solid_in.1), custom_call_target="tpu_custom_call" | custom-call | tf_op jit(solution)/shard_map/pallas_call | solution.py:358
  17.8 0.8 %shard_map.51 = (f32[15,2,16,128]{3,2,1,0:T(8,128)}, f32[19,2,16,128]{3,2,1,0:T(8,128)}) custom-call(f32[15,2,16,128]{3,2,1,0:T(8,128)S(1)} %get-tuple-element.4.phase, f32[19,2,16,128]{3,2,1,0:T(8,128)S(1)} %get-tuple-element.5.flow), custom_call_target="tpu_custom_call" | custom-call | tf_op jit(solution)/shard_map/pallas_call | solution.py:379

commit v3 on v2

--- a/solution.py
+++ b/solution.py
@@ -64,7 +64,7 @@
 
 def kernel(
     size_gx, size_gy, phase_in, flow_in, solid_in, phase_out, flow_out,
-    h_buf, f_buf, solid, slab_out, slab_in, pack_out, pack_in,
+    h_buf, f_buf, h_moved, f_moved, solid, slab_out, slab_in, pack_out, pack_in,
     load_sem, slab_send, slab_recv, pack_send, pack_recv,
 ):
     nx, nz, ny = solid.shape
@@ -75,6 +75,9 @@
     def device(side):
         return (lax.rem(gx + side[0] + size_gx, size_gx), lax.rem(gy + side[1] + size_gy, size_gy))
 
+    barrier = pltpu.get_barrier_semaphore()
+    for side in reversed(SIDES):
+        pl.semaphore_signal(barrier, inc=1, device_id=device(side), device_id_type=MESH)
     loads = [
         pltpu.make_async_copy(phase_in, h_buf.at[0], load_sem.at[0]),
         pltpu.make_async_copy(flow_in, f_buf.at[0], load_sem.at[1]),
@@ -82,9 +85,6 @@
     ]
     for load in loads:
         load.start()
-    barrier = pltpu.get_barrier_semaphore()
-    for side in SIDES:
-        pl.semaphore_signal(barrier, inc=1, device_id=device(side), device_id_type=MESH)
 
     lanes = lax.broadcasted_iota(jnp.int32, (nz, ny), 1)
     first, last = lanes == 0, lanes == ny - 1
@@ -159,6 +159,24 @@
             )
         return copies
 
+    tables = {"h": (PHASE_VELOCITIES, h_buf, h_moved), "f": (FLOW_VELOCITIES, f_buf, f_moved)}
+
+    def origin(step, kind, n, x):
+        velocities, buf, _ = tables[kind]
+        source = x - velocities[n][0]
+        side = -1 if source < 0 else 1 if source >= nx else 0
+        if side == 0:
+            return source, side, buf[step, n, source]
+        return source, side, slab_in[step, 0 if side == 1 else 1, CROSSING[-side].index((kind, n))]
+
+    def stage(step, from_slab):
+        for kind, (velocities, _, moved) in tables.items():
+            for n, (cx, cy, cz) in enumerate(velocities):
+                for x in range(nx):
+                    if (cy or cz) and (0 <= x - cx < nx) != from_slab:
+                        tile = origin(step, kind, n, x)[2]
+                        moved[n, x] = turn(turn(tile, cy, 1), cz, 0)
+
     def collide(step, own, store):
         grouped, inside, packed = own
 
@@ -169,23 +187,28 @@
             return pack_in[step, place, 1 if place == 0 else 0]
 
         def pulled(kind, n, x):
-            velocities, buf = (PHASE_VELOCITIES, h_buf) if kind == "h" else (FLOW_VELOCITIES, f_buf)
+            velocities, buf, moved = tables[kind]
             cx, cy, cz = velocities[n]
-            source = x - cx
-            side = -1 if source < 0 else 1 if source >= nx else 0
-            if side == 0:
-                tile = buf[step, n, source]
-            else:
-                tile = slab_in[step, 0 if side == 1 else 1, CROSSING[-side].index((kind, n))]
+            source, side, tile = origin(step, kind, n, x)
+            if cy or cz:
+                tile = moved[n, x]
             if cy:
-                column = from_side((side, -cy))
+                column = turned_side((side, -cy), cz)
                 slot = slots[kind, n, source - side * nx]
                 edge = 0 if cy == 1 else ny - 1
-                tile = jnp.where(lanes == edge, turn(column, edge - slot, 1), turn(tile, cy, 1))
-            return turn(tile, cz, 0)
+                tile = jnp.where(lanes == edge, turn(column, edge - slot, 1), tile)
+            return tile
+
+        turned = {}
+
+        def turned_side(side, cz):
+            if (side, cz) not in turned:
+                turned[side, cz] = turn(from_side(side), cz, 0)
+            return turned[side, cz]
 
         phase_read = [[pulled("h", n, x) for n in range(15)] for x in range(nx)]
-        field = {x: functools.reduce(jnp.add, phase_read[x]) for x in range(nx)}
+        flat_first = sorted(range(15), key=lambda n: abs(PHASE_VELOCITIES[n][1]))
+        field = {x: functools.reduce(jnp.add, [phase_read[x][n] for n in flat_first]) for x in range(nx)}
 
         def column_sum(kind, x, gy_side):
             total = None
@@ -305,25 +328,26 @@
 
     for load in loads:
         load.wait()
-    started = []
     for step in range(STEPS):
-        fill_slab(step)
+        own = pushes(step)
         if step == 0:
-            own = pushes(step)
+            fill_slab(step)
             pl.semaphore_wait(barrier, len(SIDES))
-            packs, slabs = pack_copies(step), slab_copies(step)
-            for copy in packs + slabs:
-                copy.start()
-        else:
-            slabs = slab_copies(step)
-            for copy in slabs:
-                copy.start()
-            own = pushes(step)
-            packs = pack_copies(step)
-            for copy in packs:
-                copy.start()
-        started += packs + slabs
+        packs = pack_copies(step)
+        for copy in reversed(packs):
+            copy.start()
+        if step > 0:
+            fill_slab(step)
+        slabs = slab_copies(step)
+        for copy in slabs:
+            copy.start()
+        stage(step, False)
         for copy in packs + slabs:
+            copy.wait_send()
+        for copy in slabs:
+            copy.wait_recv()
+        stage(step, True)
+        for copy in packs:
             copy.wait_recv()
 
         def store(kind, n, x, value):
@@ -333,8 +357,6 @@
                 (h_buf if kind == "h" else f_buf)[step + 1, n, x] = value
 
         collide(step, own, store)
-    for copy in started:
-        copy.wait_send()
 
 
 def write_back(phase, flow, phase_out, flow_out, sems):
@@ -363,6 +385,8 @@
         scratch_shapes=[
             pltpu.VMEM((STEPS,) + phase_pops.shape, f32),
             pltpu.VMEM((STEPS,) + flow_pops.shape, f32),
+            pltpu.VMEM(phase_pops.shape, f32),
+            pltpu.VMEM(flow_pops.shape, f32),
             pltpu.VMEM((nx, nz, ny), jnp.int32),
             pltpu.VMEM((STEPS, 2, crossing, nz, ny), f32),
             pltpu.VMEM((STEPS, 2, crossing, nz, ny), f32),

time: 18.8 us -> 18 us (0.957)
  Pallas kernels: 18 us -> 17.2 us
    pallas_call x1, Pallas kernels: 17.2 us -> 16.4 us  [shards(): pl.pallas_call(functools.partial(kernel, size_gx, size_gy), out_shape=tup...]
where the time goes in v3:
time: 18 us; the launch traced here: 17.9 us
  Pallas kernels  17.2 us (96%)
  between operations  0.64 us (4%)
    pallas_call x1, Pallas kernels, shards(): pl.pallas_call(functools.partial(kernel, size_gx, size_gy), out_shape=tup...  16.4 us
    pallas_call x1, Pallas kernels, shards(): pl.pallas_call(write_back, out_shape=tuple((jax.ShapeDtypeStruct(shape, f...  0.82 us

profile of v3, /device:TPU:0, one launch (start us, length us, event | category | flops | bytes accessed | tf_op | source)
XLA Modules:
  0.0 17.9 jit_solution(11136569771669013082)
XLA Ops:
  0.6 16.4 %shard_map.50 = (f32[15,2,16,128]{3,2,1,0:T(8,128)S(1)}, f32[19,2,16,128]{3,2,1,0:T(8,128)S(1)}) custom-call(f32[15,2,16,128]{3,2,1,0:T(8,128)} %phase_in.1, f32[19,2,16,128]{3,2,1,0:T(8,128)} %flow_in.1, s32[2,16,128]{2,1,0:T(8,128)} %solid_in.1), custom_call_target="tpu_custom_call" | custom-call | tf_op jit(solution)/shard_map/pallas_call | solution.py:380
  17.0 0.8 %shard_map.51 = (f32[15,2,16,128]{3,2,1,0:T(8,128)}, f32[19,2,16,128]{3,2,1,0:T(8,128)}) custom-call(f32[15,2,16,128]{3,2,1,0:T(8,128)S(1)} %get-tuple-element.4.phase, f32[19,2,16,128]{3,2,1,0:T(8,128)S(1)} %get-tuple-element.5.flow), custom_call_target="tpu_custom_call" | custom-call | tf_op jit(solution)/shard_map/pallas_call | solution.py:403

commit v4 on v3

--- a/solution.py
+++ b/solution.py
@@ -51,14 +51,13 @@
 
 def slot_table(nx):
     slots = {}
-    for sign in (1, -1):
+    for sign, mark in ((1, "+"), (-1, "-")):
+        keys = []
         for kind, velocities in (("h", PHASE_VELOCITIES), ("f", FLOW_VELOCITIES)):
-            for n in moving(velocities, 1, sign):
-                for x in range(nx):
-                    slots[kind, n, x] = len(slots)
-    for kind in ("edge+", "edge-", "push+", "push-"):
-        for x in range(-1, nx + 1):
-            slots[kind, x] = len(slots)
+            keys += [(kind, n, x) for n in moving(velocities, 1, sign) for x in range(nx)]
+        for kind in ("edge", "push"):
+            keys += [(kind + mark, x) for x in range(-1, nx + 1)]
+        slots.update({key: slot for slot, key in enumerate(keys)})
     return slots
 
 
@@ -69,7 +68,8 @@
 ):
     nx, nz, ny = solid.shape
     slots = slot_table(nx)
-    assert len(slots) <= ny
+    half, fold = nz // 2, ny // 2
+    assert max(slots.values()) < fold
     gx, gy = lax.axis_index("gx"), lax.axis_index("gy")
 
     def device(side):
@@ -113,7 +113,7 @@
                 + jnp.where(first, 0.0, turn(grouped[1, x], 1, 1))
                 + jnp.where(last, 0.0, turn(grouped[-1, x], -1, 1))
             )
-        packed = jnp.zeros((nz, ny), jnp.float32)
+        halves = {sign: jnp.zeros((half, ny), jnp.float32) for sign in (1, -1)}
         for key, slot in slots.items():
             if key[0] in ("h", "f"):
                 kind, n, x = key
@@ -123,7 +123,11 @@
                 sign = 1 if key[0][-1] == "+" else -1
                 tile = inside[key[1]] if key[0][:4] == "edge" else grouped[sign, key[1]]
             source = ny - 1 if sign == 1 else 0
-            packed = jnp.where(lanes == slot, turn(tile, slot - source, 1), packed)
+            for part in range(2):
+                lane = slot + part * fold
+                piece = turn(tile[part * half : (part + 1) * half], lane - source, 1)
+                halves[sign] = jnp.where(lanes[:half] == lane, piece, halves[sign])
+        packed = jnp.concatenate([halves[1], halves[-1]], axis=0)
         pack_out[step, 0] = inside[0]
         pack_out[step, 1] = packed
         pack_out[step, 2] = inside[nx - 1]
@@ -149,10 +153,11 @@
         copies = []
         for place, side in enumerate(SIDES):
             begin, length = (0, 2) if place == 0 else (1, 2) if place == 1 else (1, 1)
+            rows = pl.ds(0, nz) if side[1] == 0 else pl.ds(0 if side[1] == 1 else half, half)
             copies.append(
                 pltpu.make_async_remote_copy(
-                    pack_out.at[step, pl.ds(begin, length)],
-                    pack_in.at[step, place, pl.ds(0, length)],
+                    pack_out.at[step, pl.ds(begin, length), rows],
+                    pack_in.at[step, place, pl.ds(0, length), rows],
                     pack_send.at[step, place], pack_recv.at[step, place],
                     device_id=device(side), device_id_type=MESH,
                 )
@@ -180,11 +185,18 @@
     def collide(step, own, store):
         grouped, inside, packed = own
 
-        def from_side(side):
-            if side == (0, 0):
-                return packed
-            place = SIDES.index((-side[0], -side[1]))
-            return pack_in[step, place, 1 if place == 0 else 0]
+        unfolded = {}
+
+        def from_side(side, sign):
+            if (side, sign) not in unfolded:
+                begin = 0 if sign == 1 else half
+                if side == (0, 0):
+                    piece = packed[begin : begin + half]
+                else:
+                    place = SIDES.index((-side[0], -side[1]))
+                    piece = pack_in[step, place, 1 if place == 0 else 0, begin : begin + half]
+                unfolded[side, sign] = jnp.concatenate([piece, turn(piece, -fold, 1)], axis=0)
+            return unfolded[side, sign]
 
         def pulled(kind, n, x):
             velocities, buf, moved = tables[kind]
@@ -203,7 +215,7 @@
 
         def turned_side(side, cz):
             if (side, cz) not in turned:
-                turned[side, cz] = turn(from_side(side), cz, 0)
+                turned[side, cz] = turn(from_side(side, -side[1]), cz, 0)
             return turned[side, cz]
 
         phase_read = [[pulled("h", n, x) for n in range(15)] for x in range(nx)]
@@ -215,7 +227,7 @@
             for side in (0, 1, -1):
                 at = x - side * nx
                 if -1 <= at <= nx:
-                    value = turn(from_side((side, gy_side)), -slots[kind, at], 1)
+                    value = turn(from_side((side, gy_side), 1 if kind[-1] == "+" else -1), -slots[kind, at], 1)
                     total = value if total is None else total + value
             return total
 
@@ -226,7 +238,7 @@
                 added = None
                 for across in (0, side):
                     at = x - across * nx
-                    term = turn(from_side((across, gy_side)), where - slots[kind, at], 1)
+                    term = turn(from_side((across, gy_side), -gy_side), where - slots[kind, at], 1)
                     added = term if added is None else added + term
                 value = value + jnp.where(lanes == where, added, 0.0)
             field[x] = value

time: 18 us -> 17.9 us (level)
  no operation moved by 1% of the time
where the time goes in v4:
time: 17.9 us; the launch traced here: 17.7 us
  Pallas kernels  17.1 us (96%)
  between operations  0.64 us (4%)
    pallas_call x1, Pallas kernels, shards(): pl.pallas_call(functools.partial(kernel, size_gx, size_gy), out_shape=tup...  16.3 us
    pallas_call x1, Pallas kernels, shards(): pl.pallas_call(write_back, out_shape=tuple((jax.ShapeDtypeStruct(shape, f...  0.82 us

profile of v4, /device:TPU:0, one launch (start us, length us, event | category | flops | bytes accessed | tf_op | source)
XLA Modules:
  0.0 17.7 jit_solution(10659372069941222374)
XLA Ops:
  0.6 16.3 %shard_map.50 = (f32[15,2,16,128]{3,2,1,0:T(8,128)S(1)}, f32[19,2,16,128]{3,2,1,0:T(8,128)S(1)}) custom-call(f32[15,2,16,128]{3,2,1,0:T(8,128)} %phase_in.1, f32[19,2,16,128]{3,2,1,0:T(8,128)} %flow_in.1, s32[2,16,128]{2,1,0:T(8,128)} %solid_in.1), custom_call_target="tpu_custom_call" | custom-call | tf_op jit(solution)/shard_map/pallas_call | solution.py:392
  16.9 0.8 %shard_map.51 = (f32[15,2,16,128]{3,2,1,0:T(8,128)}, f32[19,2,16,128]{3,2,1,0:T(8,128)}) custom-call(f32[15,2,16,128]{3,2,1,0:T(8,128)S(1)} %get-tuple-element.4.phase, f32[19,2,16,128]{3,2,1,0:T(8,128)S(1)} %get-tuple-element.5.flow), custom_call_target="tpu_custom_call" | custom-call | tf_op jit(solution)/shard_map/pallas_call | solution.py:415

commit v5 on v4

--- a/solution.py
+++ b/solution.py
@@ -222,6 +222,8 @@
         flat_first = sorted(range(15), key=lambda n: abs(PHASE_VELOCITIES[n][1]))
         field = {x: functools.reduce(jnp.add, [phase_read[x][n] for n in flat_first]) for x in range(nx)}
 
+        reads = [[pulled("f", n, x) for n in range(19)] for x in range(nx)]
+
         def column_sum(kind, x, gy_side):
             total = None
             for side in (0, 1, -1):
@@ -275,7 +277,7 @@
             inv_time = 1.0 / (0.6 + 0.4 * clipped)
             potential = 4.0 * BETA * phi * (phi - 1.0) * (phi - 0.5) - KAPPA * laplacian
             force = [potential * component for component in gradient]
-            read = [pulled("f", n, x) for n in range(19)]
+            read = reads[x]
             pressure = functools.reduce(jnp.add, read)
             velocity = []
             for coordinate in range(3):

time: 17.9 us -> 17.8 us (level)
  no operation moved by 1% of the time
where the time goes in v5:
time: 17.8 us; the launch traced here: 17.6 us
  Pallas kernels  17 us (96%)
  between operations  0.64 us (4%)
    pallas_call x1, Pallas kernels, shards(): pl.pallas_call(functools.partial(kernel, size_gx, size_gy), out_shape=tup...  16.2 us
    pallas_call x1, Pallas kernels, shards(): pl.pallas_call(write_back, out_shape=tuple((jax.ShapeDtypeStruct(shape, f...  0.82 us

profile of v5, /device:TPU:0, one launch (start us, length us, event | category | flops | bytes accessed | tf_op | source)
XLA Modules:
  0.0 17.6 jit_solution(3714434398175217762)
XLA Ops:
  0.6 16.2 %shard_map.50 = (f32[15,2,16,128]{3,2,1,0:T(8,128)S(1)}, f32[19,2,16,128]{3,2,1,0:T(8,128)S(1)}) custom-call(f32[15,2,16,128]{3,2,1,0:T(8,128)} %phase_in.1, f32[19,2,16,128]{3,2,1,0:T(8,128)} %flow_in.1, s32[2,16,128]{2,1,0:T(8,128)} %solid_in.1), custom_call_target="tpu_custom_call" | custom-call | tf_op jit(solution)/shard_map/pallas_call | solution.py:394
  16.8 0.8 %shard_map.51 = (f32[15,2,16,128]{3,2,1,0:T(8,128)}, f32[19,2,16,128]{3,2,1,0:T(8,128)}) custom-call(f32[15,2,16,128]{3,2,1,0:T(8,128)S(1)} %get-tuple-element.4.phase, f32[19,2,16,128]{3,2,1,0:T(8,128)S(1)} %get-tuple-element.5.flow), custom_call_target="tpu_custom_call" | custom-call | tf_op jit(solution)/shard_map/pallas_call | solution.py:417
